TPU v7x, 256 devices: a whole 4x4x8 slice. The times are simulated.
256 devices in a mesh: row: 32 (over x_hi, z, core), col: 8 (over x_lo, y).
Axes of the slice: x: 4 (x_hi: 2, x_lo: 2; x = x_hi * 2 + x_lo), y: 4, z: 8, core: 2. Of those that a mesh axis runs over, the one named last changes fastest.
Arguments:
- amplitudes: float32 [1024, 64, 1200], P('col', 'row'), may hold values from -6 to 6
- integrals: float32 [64, 1200, 8, 1200], P('row', None, 'col'), may hold values from -0.09375 to 0.09375
- pair_energy: float32 [1024], P(('row', 'col')), may hold values from -4 to -1
- block_energy: float32 [8], replicated, may hold values from 0.2 to 3
- virtual_energy: float32 [1200], replicated, may hold values from 0.2 to 3
Outputs:
- new_amplitudes: float32 [1024, 8, 1200], P(('row', 'col'))
All inputs are finite; a program needn't handle non-finite values.
Results may differ from a plain program's by a relative error of at most 0.00027.
Values sent between devices are 32-bit elements; how exact they have to be, the bound alone decides.
A program may use at most 128 MiB of HBM per device.

v0:
```python
import jax
import jax.numpy as jnp
from jax import lax
from jax.sharding import PartitionSpec as P


def per_device(amplitudes, integrals, pair_energy, block_energy, virtual_energy):
    row_size = lax.axis_size("row")
    gathered = lax.all_gather(amplitudes, "col", axis=0, tiled=True)
    pair_count = gathered.shape[0]
    contract_len = gathered.shape[1] * gathered.shape[2]
    flattened = gathered.reshape(pair_count, contract_len)
    a_local = integrals.shape[2]
    virt_width = integrals.shape[3]
    weights = integrals.reshape(contract_len, a_local * virt_width)
    row_block = pair_count // row_size
    summed = lax.psum_scatter(
        jnp.dot(
            flattened, weights, precision=lax.Precision.HIGHEST, preferred_element_type=jnp.float32
        ),
        "row",
        scatter_dimension=0,
        tiled=True,
    )
    reshaped = summed.reshape(row_block, a_local, virt_width)
    arrived = lax.all_to_all(reshaped, "col", split_axis=0, concat_axis=1, tiled=True)
    denominator = (
        pair_energy[:, None, None] - block_energy[None, :, None] - virtual_energy[None, None, :]
    )
    return arrived / denominator


def solution(mesh):
    placed = (P("col", "row", None), P("row", None, "col", None), P(("row", "col")), P(), P())
    return jax.shard_map(
        per_device,
        mesh=mesh,
        in_specs=placed,
        out_specs=P(("row", "col"), None, None),
        check_vma=False,
    )
```

profile of v0, /device:TPU:1, one launch (start us, length us, event | category | flops | bytes accessed | tf_op | source)
XLA Modules:
  0.0 323.8 jit_solution(6195841070064501322)
XLA Ops:
  6.5 0.0 all-gather.2.cloned.1.call-start
  6.5 0.7 all-gather.2.cloned.1.call-update
  7.3 0.0 reduce-scatter.2.cloned.1.call-start
  7.3 9.8 %copy.10 = f32[2,1200,1,1200]{3,1,2,0:T(8,128)} copy(f32[2,1200,1,1200]{3,2,1,0:T(1,128)} %param.6) | data formatting | bytes 23040000
  17.1 106.9 %all-gather.2.cloned.1.call-done = f32[1024,2,1200]{0,2,1:T(8,128)} async-done(((f32[128,2,1200]{0,2,1:T(8,128)}), f32[1024,2,1200]{0,2,1:T(8,128)}) %all-gather.2.cloned.1.call-update) | async-done | bytes 9830416 | tf_op jit(solution)/shard_map/all_gather | solution.py:9
  124.0 0.0 copy-start.1
  124.0 0.0 copy-start.2
  124.0 0.0 copy-start
  124.0 47.6 %fusion = f32[1024,1200]{1,0:T(8,128)} fusion(f32[1024,2400]{0,1:T(8,128)} %bitcast.13, f32[2400,1200]{1,0:T(8,128)} %bitcast.10), kind=kOutput, calls=%fused_computation.2 | convolution fusion | flops 35389440000 | bytes 26265600 | tf_op jit(solution)/shard_map/dot_general | solution.py:18
  171.6 0.0 reduce-scatter.2.cloned.1.call-update
  171.6 132.6 %reduce-scatter.2.cloned.1.call-done = f32[32,1200]{1,0:T(8,128)} async-done(((f32[1024,1200]{1,0:T(8,128)}), f32[32,1200]{1,0:T(8,128)}) %reduce-scatter.2.cloned.1.call-update) | async-done | bytes 153616 | tf_op jit(solution)/shard_map/reduce_scatter | solution.py:17
  304.2 1.7 copy.8
  306.0 4.6 %all-to-all-start = ((f32[32,1,1200]{2,1,0:T(1,128)}), f32[32,1,1200]{2,1,0:T(1,128)S(1)}, u32[]{:S(2)}, u32[]{:S(2)}) async-start(f32[32,1,1200]{2,1,0:T(1,128)} %copy.8), calls=%async_computation.1 | async-start | bytes 327680 | tf_op jit(solution)/shard_map/all_to_all | solution.py:26
  310.6 0.0 copy-done.1
  310.6 0.0 copy-done.2
  310.6 0.1 broadcast_subtract_fusion
  310.7 5.5 %all-to-all-done = f32[32,1,1200]{2,1,0:T(1,128)S(1)} async-done(((f32[32,1,1200]{2,1,0:T(1,128)}), f32[32,1,1200]{2,1,0:T(1,128)S(1)}, u32[]{:S(2)}, u32[]{:S(2)}) %all-to-all-start) | async-done | bytes 153632 | tf_op jit(solution)/shard_map/all_to_all | solution.py:26
  316.2 0.0 copy-done
  316.2 0.8 bitcast_divide_fusion
Async XLA Ops:
  6.5 117.4 %all-gather.2.cloned.1.call-start = ((), (), s32[]{:S(2)}) async-start(), calls=%async_computation.2 | async-start | bytes 11059200 | tf_op jit(solution)/shard_map/all_gather | solution.py:9
  7.3 297.0 %reduce-scatter.2.cloned.1.call-start = ((), (), s32[]{:S(2)}) async-start(), calls=%async_computation.3 | async-start | bytes 5406720 | tf_op jit(solution)/shard_map/reduce_scatter | solution.py:17
  124.0 186.6 %copy-start.1 = (f32[8]{0:T(128)S(1)}, f32[8]{0:T(128)}, u32[]{:S(2)}) copy-start(f32[8]{0:T(128)} %param.8) | copy-start | bytes 100
  124.0 186.6 %copy-start.2 = (f32[4]{0:T(128)S(1)}, f32[4]{0:T(128)}, u32[]{:S(2)}) copy-start(f32[4]{0:T(128)} %param.7) | copy-start | bytes 52
  124.0 192.2 %copy-start = (f32[1200]{0:T(1024)S(1)}, f32[1200]{0:T(1024)}, u32[]{:S(2)}) copy-start(f32[1200]{0:T(1024)} %param.9) | copy-start | bytes 14404
  306.0 10.2 %all-to-all-start = ((f32[32,1,1200]{2,1,0:T(1,128)}), f32[32,1,1200]{2,1,0:T(1,128)S(1)}, u32[]{:S(2)}, u32[]{:S(2)}) async-start(f32[32,1,1200]{2,1,0:T(1,128)} %copy.8), calls=%async_computation.1 | async-start | bytes 327680 | tf_op jit(solution)/shard_map/all_to_all | solution.py:26
Sparse Core Ops, SparseCore 0:
  9.1 114.8 all-gather.1
  171.7 132.4 reduce-scatter.1
where the time goes:
time: 328 us; the launch traced here: 324 us
  waiting for transfers between devices  246 us (75%)
  matrix products  47.6 us (15%)
  between operations  13.4 us (4%)
  local copies, waits for them, and re-layouts  11.5 us (4%)
  starting transfers between devices  4.64 us (1%)
    reduce_scatter x1, waiting for transfers between devices, per_device(): lax.psum_scatter(jnp.dot(flattened, weights, precision=lax.Precision.HIGH...  133 us
    all_gather x1, waiting for transfers between devices, per_device(): gathered = lax.all_gather(amplitudes, 'col', axis=0, tiled=True)  107 us
    dot_general x1, matrix products, per_device(): jnp.dot(flattened, weights, precision=lax.Precision.HIGHEST, preferred_el...  47.6 us
    unnamed x7, local copies, waits for them, and re-layouts  9.78 us
  transfers between devices with their start and end apart: 3, of which 3 were waited for; matrix products, arithmetic and copies ran while one was open for 3% of the time, Pallas kernels for 0%

commit v1 on v0

v1 whole, which is shorter than its diff:
```python
import functools

import jax
import jax.numpy as jnp
from jax import lax
from jax.experimental import pallas as pl
from jax.experimental.pallas import tpu as pltpu
from jax.sharding import PartitionSpec as P

MESH = pl.DeviceIdType.MESH

OWN, LEFT, RIGHT, ACROSS, ACROSS_LEFT, ACROSS_RIGHT, FAR, ACROSS_FAR = range(8)
Y_SIZE, Z_SIZE = 4, 8
PAIRS = 128
WIDTH = 1200
PADDED = 1280
HALF = PADDED // 2
DEPTH = 2400
TILE = 480
TILES = DEPTH // TILE
TILE_PAD = 512
STAGE = 240
STAGES = DEPTH // STAGE
SLOTS = 4
SPLIT = 3 * TILE
FIRST = (0, SPLIT)
SECOND = (SPLIT, DEPTH - SPLIT)
BLOCK = PAIRS // Z_SIZE
PART = BLOCK // 2
QUAD = 4
COLUMN = 256


def halves(rows):
    start, size = rows
    return (start, size // 2), (start + size // 2, size // 2)


def kernel(
    amp_ref,
    int_ref,
    pair_ref,
    block_ref,
    virt_ref,
    out_ref,
    gathered,
    stage,
    b_high,
    b_low,
    lhs,
    partial,
    core_in,
    summed,
    z_in,
    z_sum,
    x_in,
    quads,
    final,
    own_sem,
    stage_sem,
    up_send,
    up_recv,
    down_send,
    down_recv,
    over_send,
    over_recv,
    core_send,
    core_recv,
    z_send,
    z_recv,
    x_send,
    x_recv,
    final_send,
    final_recv,
):
    row = lax.axis_index("row")
    col = lax.axis_index("col")
    x_hi, z, core = row // 16, (row // 2) % Z_SIZE, row % 2
    x_lo, y = col // Y_SIZE, col % Y_SIZE

    up = {"row": row, "col": x_lo * Y_SIZE + (y + 1) % Y_SIZE}
    down = {"row": row, "col": x_lo * Y_SIZE + (y + 3) % Y_SIZE}
    over = {"row": row, "col": (1 - x_lo) * Y_SIZE + y}
    partner = {"row": row + 1 - 2 * core, "col": col}
    opposite = {"row": row + 16 - 32 * x_hi, "col": col}

    def at_z(step):
        return {"row": x_hi * 16 + ((z + step) % Z_SIZE) * 2 + core, "col": col}

    def load(index):
        slot = index % SLOTS
        source = int_ref.at[index // 5, pl.ds((index % 5) * STAGE, STAGE), 0]
        return pltpu.make_async_copy(source, stage.at[slot], stage_sem.at[slot])

    own_copy = pltpu.make_async_copy(amp_ref, gathered.at[OWN], own_sem)
    for index in range(SLOTS):
        load(index).start()

    barrier = pltpu.get_barrier_semaphore()

    def greet(device):
        pl.semaphore_signal(barrier, inc=1, device_id=device, device_id_type=MESH)

    for device in (up, down, over, partner, opposite):
        greet(device)
    for step in range(1, Z_SIZE):
        greet(at_z(step))
    source_z = 2 * (row % 4) + col // 4
    source_row = ((col % 4) // 2) * 16 + source_z * 2
    for other_col in range(8):
        for other_core in range(2):
            greet({"row": source_row + other_core, "col": other_col})
    own_copy.start()
    pl.semaphore_wait(barrier, 5 + 7 + 16)

    sends = []

    def send(source, target, send_sem, recv_sem, device):
        copy = pltpu.make_async_remote_copy(
            src_ref=source,
            dst_ref=target,
            send_sem=send_sem,
            recv_sem=recv_sem,
            device_id=device,
            device_id_type=MESH,
        )
        copy.start()
        return copy

    def landed(ref, sem):
        pltpu.make_async_copy(ref, ref, sem).wait()

    counts = {"up": 0, "down": 0, "over": 0}
    lanes = {
        "up": (up, up_send, up_recv),
        "down": (down, down_send, down_recv),
        "over": (over, over_send, over_recv),
    }
    arrivals = {}

    def forward(lane, source, target, rows):
        device, send_sem, recv_sem = lanes[lane]
        index = counts[lane]
        counts[lane] = index + 1
        start, size = rows
        if source == OWN:
            source_ref = amp_ref.at[pl.ds(start, size)]
        else:
            source_ref = gathered.at[source, pl.ds(start, size)]
        target_ref = gathered.at[target, pl.ds(start, size)]
        sends.append(send(source_ref, target_ref, send_sem.at[index], recv_sem.at[index], device))
        arrivals[(lane, target, rows)] = (target_ref, recv_sem.at[index])

    def arrived(lane, target, rows):
        landed(*arrivals.pop((lane, target, rows)))

    low_half, high_half = range(2)
    second_halves, first_halves = halves(SECOND), halves(FIRST)

    forward("up", OWN, LEFT, SECOND)
    forward("down", OWN, RIGHT, SECOND)
    forward("over", OWN, ACROSS, FIRST)
    forward("up", OWN, LEFT, FIRST)
    forward("down", OWN, RIGHT, FIRST)
    forward("over", OWN, ACROSS, SECOND)

    for tile in range(TILES):
        zeros = jnp.zeros((TILE_PAD - TILE, PADDED), jnp.bfloat16)
        b_high[pl.ds(tile * TILE_PAD + TILE, TILE_PAD - TILE), :] = zeros
        b_low[pl.ds(tile * TILE_PAD + TILE, TILE_PAD - TILE), :] = zeros

    def prepare(index, carry):
        load(index).wait()
        value = stage[index % SLOTS]
        high = value.astype(jnp.bfloat16)
        low = (value - high.astype(jnp.float32)).astype(jnp.bfloat16)
        start = pl.multiple_of((index // 2) * TILE_PAD + (index % 2) * STAGE, 16)
        b_high[pl.ds(start, STAGE), pl.ds(0, WIDTH)] = high
        b_low[pl.ds(start, STAGE), pl.ds(0, WIDTH)] = low

        @pl.when(index + SLOTS < STAGES)
        def _():
            load(index + SLOTS).start()

        return carry

    def split(slot, place, places, first, last):
        def body(tile, carry):
            value = gathered[slot, pl.ds(pl.multiple_of(tile * TILE, 8), TILE), :]
            value = jnp.concatenate([value, jnp.zeros((TILE_PAD - TILE, PAIRS), jnp.float32)], axis=0).T
            high = value.astype(jnp.bfloat16)
            low = (value - high.astype(jnp.float32)).astype(jnp.bfloat16)
            lanes_of = pl.ds(pl.multiple_of(tile * TILE_PAD, TILE_PAD), TILE_PAD)
            lhs[pl.ds(place * PAIRS, PAIRS), lanes_of] = high
            lhs[pl.ds((places + place) * PAIRS, PAIRS), lanes_of] = low
            return carry

        lax.fori_loop(first, last, body, 0)

    def multiply(slots, first, last, add):
        places = len(slots)
        rows = places * PAIRS
        for place, slot in enumerate(slots):
            split(slot, place, places, first, last)
        depth = pl.ds(first * TILE_PAD, (last - first) * TILE_PAD)

        def body(step, carry):
            columns = pl.ds(pl.multiple_of(step * COLUMN, COLUMN), COLUMN)
            both = jnp.dot(lhs[pl.ds(0, 2 * rows), depth], b_high[depth, columns], preferred_element_type=jnp.float32)
            rest = jnp.dot(lhs[pl.ds(0, rows), depth], b_low[depth, columns], preferred_element_type=jnp.float32)
            total = both[:rows] + (both[rows:] + rest)
            for place, slot in enumerate(slots):
                piece = total[place * PAIRS : (place + 1) * PAIRS]
                if add:
                    piece = piece + partial[slot, :, columns]
                partial[slot, :, columns] = piece
            return carry

        lax.fori_loop(0, PADDED // COLUMN, body, 0)

    kept = pl.ds(pl.multiple_of(core * HALF, 128), HALF)
    given = pl.ds(pl.multiple_of((1 - core) * HALF, 128), HALF)

    def to_core(slot):
        sends.append(
            send(partial.at[slot, :, given], core_in.at[slot], core_send.at[slot], core_recv.at[slot], partner)
        )

    def to_z(slot):
        landed(core_in.at[slot], core_recv.at[slot])
        summed[slot] = partial[slot, :, kept] + core_in[slot]
        for step in range(1, Z_SIZE):
            start = pl.multiple_of(((z + step) % Z_SIZE) * BLOCK, BLOCK)
            send(
                summed.at[slot, pl.ds(start, BLOCK)],
                z_in.at[slot, step - 1],
                z_send.at[slot],
                z_recv.at[slot],
                at_z(step),
            )

    def to_x(slot):
        landed(z_in.at[slot], z_recv.at[slot])
        total = summed[slot, pl.ds(pl.multiple_of(z * BLOCK, BLOCK), BLOCK), :]
        for step in range(Z_SIZE - 1):
            total = total + z_in[slot, step]
        z_sum[slot] = total
        start = pl.multiple_of((1 - x_hi) * PART, PART)
        sends.append(
            send(z_sum.at[slot, pl.ds(start, PART)], x_in.at[slot], x_send.at[slot], x_recv.at[slot], opposite)
        )

    def chunk_col(slot):
        shift = {OWN: 0, LEFT: 3, RIGHT: 1, ACROSS: 0, ACROSS_LEFT: 3, ACROSS_RIGHT: 1, FAR: 2, ACROSS_FAR: 2}[slot]
        side = x_lo if slot in (OWN, LEFT, RIGHT, FAR) else 1 - x_lo
        return side * Y_SIZE + (y + shift) % Y_SIZE

    owners = []

    def to_owner(slot):
        landed(x_in.at[slot], x_recv.at[slot])
        total = z_sum[slot, pl.ds(pl.multiple_of(x_hi * PART, PART), PART), :] + x_in[slot]
        owner_row = 4 * chunk_col(slot) + z // 2
        for quad in range(2):
            quads[slot, quad] = total[quad * QUAD : (quad + 1) * QUAD]
            owner_col = 4 * (z % 2) + 2 * x_hi + quad
            here = jnp.logical_and(owner_row == row, owner_col == col)
            source, target = quads.at[slot, quad], final.at[col, core]
            copy = pltpu.make_async_remote_copy(
                src_ref=source,
                dst_ref=target,
                send_sem=final_send.at[slot, quad],
                recv_sem=final_recv,
                device_id={"row": owner_row, "col": owner_col},
                device_id_type=MESH,
            )

            @pl.when(here)
            def _(source=source, target=target):
                pltpu.make_async_copy(source, target, final_recv).start()

            @pl.when(jnp.logical_not(here))
            def _(copy=copy):
                copy.start()

            owners.append((here, copy))

    lax.fori_loop(0, STAGES // 2, prepare, 0)

    arrived("up", LEFT, SECOND)
    forward("up", LEFT, FAR, second_halves[low_half])
    forward("over", LEFT, ACROSS_LEFT, SECOND)
    arrived("down", RIGHT, SECOND)
    forward("down", RIGHT, FAR, second_halves[high_half])
    forward("over", RIGHT, ACROSS_RIGHT, SECOND)
    arrived("over", ACROSS, FIRST)
    forward("up", ACROSS, ACROSS_LEFT, FIRST)
    forward("down", ACROSS, ACROSS_RIGHT, FIRST)

    lax.fori_loop(STAGES // 2, STAGES, prepare, 0)

    own_copy.wait()
    multiply((OWN,), 0, TILES, False)
    to_core(OWN)

    arrived("up", LEFT, FIRST)
    forward("up", LEFT, FAR, first_halves[low_half])
    arrived("down", RIGHT, FIRST)
    forward("down", RIGHT, FAR, first_halves[high_half])
    to_z(OWN)
    multiply((LEFT, RIGHT), 0, TILES, False)
    to_core(LEFT)
    to_core(RIGHT)

    arrived("up", FAR, second_halves[low_half])
    arrived("down", FAR, second_halves[high_half])
    forward("over", FAR, ACROSS_FAR, SECOND)
    to_x(OWN)
    to_z(LEFT)
    to_z(RIGHT)

    arrived("over", ACROSS, SECOND)
    multiply((ACROSS,), 0, TILES, False)
    to_core(ACROSS)
    to_owner(OWN)
    to_x(LEFT)
    to_x(RIGHT)
    to_z(ACROSS)

    arrived("up", ACROSS_LEFT, FIRST)
    forward("up", ACROSS_LEFT, ACROSS_FAR, first_halves[low_half])
    arrived("down", ACROSS_RIGHT, FIRST)
    forward("down", ACROSS_RIGHT, ACROSS_FAR, first_halves[high_half])
    arrived("over", ACROSS_LEFT, SECOND)
    arrived("over", ACROSS_RIGHT, SECOND)
    multiply((ACROSS_LEFT, ACROSS_RIGHT), 0, TILES, False)
    to_core(ACROSS_LEFT)
    to_core(ACROSS_RIGHT)
    to_owner(LEFT)
    to_owner(RIGHT)
    to_x(ACROSS)

    arrived("up", FAR, first_halves[low_half])
    arrived("down", FAR, first_halves[high_half])
    to_z(ACROSS_LEFT)
    to_z(ACROSS_RIGHT)
    multiply((FAR,), 0, TILES, False)
    to_core(FAR)
    to_owner(ACROSS)

    arrived("over", ACROSS_FAR, SECOND)
    multiply((ACROSS_FAR,), SPLIT // TILE, TILES, False)
    to_z(FAR)
    arrived("up", ACROSS_FAR, first_halves[low_half])
    arrived("down", ACROSS_FAR, first_halves[high_half])
    multiply((ACROSS_FAR,), 0, SPLIT // TILE, True)
    to_core(ACROSS_FAR)
    to_x(ACROSS_LEFT)
    to_x(ACROSS_RIGHT)
    to_z(ACROSS_FAR)
    to_owner(ACROSS_LEFT)
    to_owner(ACROSS_RIGHT)
    to_x(FAR)
    to_owner(FAR)
    to_x(ACROSS_FAR)
    to_owner(ACROSS_FAR)

    landed(final, final_recv)
    for orbital in range(8):
        for side in range(2):
            size = min(WIDTH - side * HALF, HALF)
            for pair in range(QUAD):
                base = pair_ref[pair] - block_ref[orbital]
                below = base - virt_ref[:, pl.ds(side * HALF, size)]
                out_ref[pl.ds(pair, 1), orbital, pl.ds(side * HALF, size)] = (
                    final[orbital, side, pl.ds(pair, 1), pl.ds(0, size)] / below
                )

    for copy in sends:
        copy.wait_send()
    for slot in range(8):
        landed(z_in.at[slot], z_send.at[slot])
    for here, copy in owners:

        @pl.when(jnp.logical_not(here))
        def _(copy=copy):
            copy.wait_send()


def per_device(amplitudes, integrals, pair_energy, block_energy, virtual_energy):
    shard = jnp.transpose(amplitudes, (1, 2, 0)).reshape(DEPTH, PAIRS)
    f32, b16 = jnp.float32, jnp.bfloat16
    dma = pltpu.SemaphoreType.DMA
    return pl.pallas_call(
        kernel,
        out_shape=jax.ShapeDtypeStruct((QUAD, 8, WIDTH), f32),
        in_specs=[
            pl.BlockSpec(memory_space=pl.ANY),
            pl.BlockSpec(memory_space=pl.ANY),
            pl.BlockSpec(memory_space=pltpu.SMEM),
            pl.BlockSpec(memory_space=pltpu.SMEM),
            pl.BlockSpec(memory_space=pltpu.VMEM),
        ],
        out_specs=pl.BlockSpec(memory_space=pltpu.VMEM),
        scratch_shapes=[
            pltpu.VMEM((8, DEPTH, PAIRS), f32),
            pltpu.VMEM((SLOTS, STAGE, WIDTH), f32),
            pltpu.VMEM((TILES * TILE_PAD, PADDED), b16),
            pltpu.VMEM((TILES * TILE_PAD, PADDED), b16),
            pltpu.VMEM((4 * PAIRS, TILES * TILE_PAD), b16),
            pltpu.VMEM((8, PAIRS, PADDED), f32),
            pltpu.VMEM((8, PAIRS, HALF), f32),
            pltpu.VMEM((8, PAIRS, HALF), f32),
            pltpu.VMEM((8, Z_SIZE - 1, BLOCK, HALF), f32),
            pltpu.VMEM((8, BLOCK, HALF), f32),
            pltpu.VMEM((8, PART, HALF), f32),
            pltpu.VMEM((8, 2, QUAD, HALF), f32),
            pltpu.VMEM((8, 2, QUAD, HALF), f32),
            dma,
            dma((SLOTS,)),
            dma((6,)),
            dma((6,)),
            dma((6,)),
            dma((6,)),
            dma((5,)),
            dma((5,)),
            dma((8,)),
            dma((8,)),
            dma((8,)),
            dma((8,)),
            dma((8,)),
            dma((8,)),
            dma((8, 2)),
            dma,
        ],
        compiler_params=pltpu.CompilerParams(
            collective_id=0, has_side_effects=True, vmem_limit_bytes=62 * 1024 * 1024
        ),
    )(shard, integrals, pair_energy, block_energy, virtual_energy.reshape(1, WIDTH))


def solution(mesh):
    placed = (P("col", "row", None), P("row", None, "col", None), P(("row", "col")), P(), P())
    return jax.shard_map(
        per_device,
        mesh=mesh,
        in_specs=placed,
        out_specs=P(("row", "col"), None, None),
        check_vma=False,
    )
```

time: 328 us -> 128 us (0.39); the launches traced: 324 us -> 128 us
  waiting for transfers between devices: 246 us -> 0 us
  Pallas kernels: 0 us -> 125 us
  matrix products: 47.6 us -> 0 us
  between operations: 13.4 us -> 0.01 us
  local copies, waits for them, and re-layouts: 11.5 us -> 2.89 us
  starting transfers between devices: 4.64 us -> 0 us
    reduce_scatter x1 -> x0, waiting for transfers between devices: 133 us -> none  [per_device(): lax.psum_scatter(jnp.dot(flattened, weights, precision=lax.Precision.HIGH...]
    pallas_call x0 -> x1, Pallas kernels: none -> 125 us  [per_device(): pl.pallas_call(kernel, out_shape=jax.ShapeDtypeStruct((QUAD, 8, WIDTH), f...]
    all_gather x1 -> x0, waiting for transfers between devices: 107 us -> none  [per_device(): gathered = lax.all_gather(amplitudes, 'col', axis=0, tiled=True)]
    dot_general x1 -> x0, matrix products: 47.6 us -> none  [per_device(): jnp.dot(flattened, weights, precision=lax.Precision.HIGHEST, preferred_el...]
    unnamed x7 -> x1, local copies, waits for them, and re-layouts: 9.78 us -> 1.59 us
    all_to_all x1 -> x0, waiting for transfers between devices: 5.52 us -> none  [per_device(): lax.all_to_all(reshaped, 'col', split_axis=0, concat_axis=1, tiled=True)]
    all_to_all x1 -> x0, starting transfers between devices: 4.6 us -> none  [per_device(): lax.all_to_all(reshaped, 'col', split_axis=0, concat_axis=1, tiled=True)]
  transfers between devices with their start and end apart: 3 -> 0, of which waited for: 3 -> 0; matrix products, arithmetic and copies ran while one was open for 3% -> 0% of each run, Pallas kernels for 0% -> 0%
where the time goes in v1:
time: 128 us
  Pallas kernels  125 us (98%)
  local copies, waits for them, and re-layouts  2.89 us (2%)
    pallas_call x1, Pallas kernels, per_device(): pl.pallas_call(kernel, out_shape=jax.ShapeDtypeStruct((QUAD, 8, WIDTH), f...  125 us

profile of v1, /device:TPU:1, one launch (start us, length us, event | category | flops | bytes accessed | tf_op | source)
XLA Modules:
  0.0 127.7 jit_solution(14628276615603085833)
XLA Ops:
  0.0 1.3 %reshape.7.virt_ref = f32[1,1200]{1,0:T(1,128)} reshape(f32[1200]{0:T(1024)} %param.9) | data formatting | bytes 9600 | tf_op jit(solution)/shard_map/reshape | solution.py:439
  1.3 124.8 %shard_map.55 = f32[4,8,1200]{2,1,0:T(8,128)} custom-call(f32[2400,128]{1,0:T(8,128)} %bitcast.3, f32[2,1200,1,1200]{3,2,1,0:T(1,128)} %int_ref.1, f32[4]{0:T(128)} %pair_ref.1, f32[8]{0:T(128)} %block_ref.1, f32[1,1200]{1,0:T(1,128)} %reshape.7.virt_ref), custom_call_target="tpu_custom_call" | custom-call | tf_op jit(solution)/shard_map/pallas_call | solution.py:394
  126.1 1.6 %copy.7 = f32[4,8,1200]{2,1,0:T(8,128)} copy(f32[4,8,1200]{2,1,0:T(8,128)} %shard_map.55) | data formatting | bytes 307200

commit v2 on v1

--- a/solution.py
+++ b/solution.py
@@ -28,6 +28,8 @@
 BLOCK = PAIRS // Z_SIZE
 PART = BLOCK // 2
 QUAD = 4
+LONG, SHORT = 0, 1
+HOPS = (4, 3)
 COLUMN = 256
 
 
@@ -103,7 +105,7 @@
 
     for device in (up, down, over, partner, opposite):
         greet(device)
-    for step in range(1, Z_SIZE):
+    for step in (1, Z_SIZE - 1):
         greet(at_z(step))
     source_z = 2 * (row % 4) + col // 4
     source_row = ((col % 4) // 2) * 16 + source_z * 2
@@ -111,7 +113,7 @@
         for other_core in range(2):
             greet({"row": source_row + other_core, "col": other_col})
     own_copy.start()
-    pl.semaphore_wait(barrier, 5 + 7 + 16)
+    pl.semaphore_wait(barrier, 5 + 2 + 16)
 
     sends = []
 
@@ -229,21 +231,39 @@
     def to_z(slot):
         landed(core_in.at[slot], core_recv.at[slot])
         summed[slot] = partial[slot, :, kept] + core_in[slot]
-        for step in range(1, Z_SIZE):
-            start = pl.multiple_of(((z + step) % Z_SIZE) * BLOCK, BLOCK)
-            send(
-                summed.at[slot, pl.ds(start, BLOCK)],
-                z_in.at[slot, step - 1],
-                z_send.at[slot],
-                z_recv.at[slot],
-                at_z(step),
-            )
+        along(slot, LONG, 0)
+        along(slot, SHORT, 0)
+
+    def block_at(step):
+        return pl.ds(pl.multiple_of(((z + step) % Z_SIZE) * BLOCK, BLOCK), BLOCK)
+
+    def along(slot, chain, hop):
+        way = (1 if slot % 2 == 0 else -1) * (1 if chain == LONG else -1)
+        block = block_at(way * (HOPS[chain] - hop) + Z_SIZE)
+        place = chain * HOPS[LONG] + hop
+        if hop:
+            came = z_in.at[slot, place - 1]
+            landed(came, z_recv.at[slot, place - 1])
+            summed[slot, block] = summed[slot, block] + came[...]
+        send(
+            summed.at[slot, block],
+            z_in.at[slot, place],
+            z_send.at[slot],
+            z_recv.at[slot, place],
+            at_z(way + Z_SIZE),
+        )
+
+    def z_step(slot, hop):
+        along(slot, LONG, hop)
+        if hop < HOPS[SHORT]:
+            along(slot, SHORT, hop)
 
     def to_x(slot):
-        landed(z_in.at[slot], z_recv.at[slot])
-        total = summed[slot, pl.ds(pl.multiple_of(z * BLOCK, BLOCK), BLOCK), :]
-        for step in range(Z_SIZE - 1):
-            total = total + z_in[slot, step]
+        total = summed[slot, block_at(0)]
+        for chain in (SHORT, LONG):
+            place = chain * HOPS[LONG] + HOPS[chain] - 1
+            landed(z_in.at[slot, place], z_recv.at[slot, place])
+            total = total + z_in[slot, place]
         z_sum[slot] = total
         start = pl.multiple_of((1 - x_hi) * PART, PART)
         sends.append(
@@ -285,6 +305,27 @@
 
             owners.append((here, copy))
 
+    active = []
+
+    def reduce(*slots):
+        for slot in slots:
+            to_core(slot)
+            active.append([slot, 0])
+
+    def pump():
+        for entry in list(active):
+            slot, stage_of = entry
+            if stage_of == 0:
+                to_z(slot)
+            elif stage_of < HOPS[LONG]:
+                z_step(slot, stage_of)
+            elif stage_of == HOPS[LONG]:
+                to_x(slot)
+            else:
+                to_owner(slot)
+                active.remove(entry)
+            entry[1] = stage_of + 1
+
     lax.fori_loop(0, STAGES // 2, prepare, 0)
 
     arrived("up", LEFT, SECOND)
@@ -301,69 +342,54 @@
 
     own_copy.wait()
     multiply((OWN,), 0, TILES, False)
-    to_core(OWN)
+    reduce(OWN)
 
     arrived("up", LEFT, FIRST)
     forward("up", LEFT, FAR, first_halves[low_half])
     arrived("down", RIGHT, FIRST)
     forward("down", RIGHT, FAR, first_halves[high_half])
-    to_z(OWN)
+    pump()
     multiply((LEFT, RIGHT), 0, TILES, False)
-    to_core(LEFT)
-    to_core(RIGHT)
+    reduce(LEFT, RIGHT)
+    pump()
 
     arrived("up", FAR, second_halves[low_half])
     arrived("down", FAR, second_halves[high_half])
     forward("over", FAR, ACROSS_FAR, SECOND)
-    to_x(OWN)
-    to_z(LEFT)
-    to_z(RIGHT)
-
     arrived("over", ACROSS, SECOND)
     multiply((ACROSS,), 0, TILES, False)
-    to_core(ACROSS)
-    to_owner(OWN)
-    to_x(LEFT)
-    to_x(RIGHT)
-    to_z(ACROSS)
+    reduce(ACROSS)
+    pump()
+    pump()
+    pump()
 
     arrived("up", ACROSS_LEFT, FIRST)
     forward("up", ACROSS_LEFT, ACROSS_FAR, first_halves[low_half])
     arrived("down", ACROSS_RIGHT, FIRST)
     forward("down", ACROSS_RIGHT, ACROSS_FAR, first_halves[high_half])
+    pump()
     arrived("over", ACROSS_LEFT, SECOND)
     arrived("over", ACROSS_RIGHT, SECOND)
     multiply((ACROSS_LEFT, ACROSS_RIGHT), 0, TILES, False)
-    to_core(ACROSS_LEFT)
-    to_core(ACROSS_RIGHT)
-    to_owner(LEFT)
-    to_owner(RIGHT)
-    to_x(ACROSS)
+    reduce(ACROSS_LEFT, ACROSS_RIGHT)
+    pump()
 
     arrived("up", FAR, first_halves[low_half])
     arrived("down", FAR, first_halves[high_half])
-    to_z(ACROSS_LEFT)
-    to_z(ACROSS_RIGHT)
+    pump()
     multiply((FAR,), 0, TILES, False)
-    to_core(FAR)
-    to_owner(ACROSS)
+    reduce(FAR)
+    pump()
 
     arrived("over", ACROSS_FAR, SECOND)
     multiply((ACROSS_FAR,), SPLIT // TILE, TILES, False)
-    to_z(FAR)
+    pump()
     arrived("up", ACROSS_FAR, first_halves[low_half])
     arrived("down", ACROSS_FAR, first_halves[high_half])
     multiply((ACROSS_FAR,), 0, SPLIT // TILE, True)
-    to_core(ACROSS_FAR)
-    to_x(ACROSS_LEFT)
-    to_x(ACROSS_RIGHT)
-    to_z(ACROSS_FAR)
-    to_owner(ACROSS_LEFT)
-    to_owner(ACROSS_RIGHT)
-    to_x(FAR)
-    to_owner(FAR)
-    to_x(ACROSS_FAR)
-    to_owner(ACROSS_FAR)
+    reduce(ACROSS_FAR)
+    while active:
+        pump()
 
     landed(final, final_recv)
     for orbital in range(8):
@@ -427,7 +453,7 @@
             dma((8,)),
             dma((8,)),
             dma((8,)),
-            dma((8,)),
+            dma((8, Z_SIZE - 1)),
             dma((8,)),
             dma((8,)),
             dma((8, 2)),

time: 128 us -> 127 us (level)
  no operation moved by 1% of the time
where the time goes in v2:
time: 127 us
  Pallas kernels  124 us (98%)
  local copies, waits for them, and re-layouts  2.89 us (2%)
    pallas_call x1, Pallas kernels, per_device(): pl.pallas_call(kernel, out_shape=jax.ShapeDtypeStruct((QUAD, 8, WIDTH), f...  124 us

profile of v2, /device:TPU:1, one launch (start us, length us, event | category | flops | bytes accessed | tf_op | source)
XLA Modules:
  0.0 127.0 jit_solution(11777232803374357981)
XLA Ops:
  0.0 1.3 %reshape.7.virt_ref = f32[1,1200]{1,0:T(1,128)} reshape(f32[1200]{0:T(1024)} %param.9) | data formatting | bytes 9600 | tf_op jit(solution)/shard_map/reshape | solution.py:465
  1.3 124.1 %shard_map.55 = f32[4,8,1200]{2,1,0:T(8,128)} custom-call(f32[2400,128]{1,0:T(8,128)} %bitcast.3, f32[2,1200,1,1200]{3,2,1,0:T(1,128)} %int_ref.1, f32[4]{0:T(128)} %pair_ref.1, f32[8]{0:T(128)} %block_ref.1, f32[1,1200]{1,0:T(1,128)} %reshape.7.virt_ref), custom_call_target="tpu_custom_call" | custom-call | tf_op jit(solution)/shard_map/pallas_call | solution.py:420
  125.4 1.6 %copy.7 = f32[4,8,1200]{2,1,0:T(8,128)} copy(f32[4,8,1200]{2,1,0:T(8,128)} %shard_map.55) | data formatting | bytes 307200

commit v3 on v2

--- a/solution.py
+++ b/solution.py
@@ -312,9 +312,11 @@
             to_core(slot)
             active.append([slot, 0])
 
-    def pump():
+    def pump(last=False):
         for entry in list(active):
             slot, stage_of = entry
+            if stage_of > HOPS[LONG] and not last:
+                continue
             if stage_of == 0:
                 to_z(slot)
             elif stage_of < HOPS[LONG]:
@@ -389,7 +391,7 @@
     multiply((ACROSS_FAR,), 0, SPLIT // TILE, True)
     reduce(ACROSS_FAR)
     while active:
-        pump()
+        pump(True)
 
     landed(final, final_recv)
     for orbital in range(8):

time: 127 us -> 122 us (0.961)
  Pallas kernels: 124 us -> 118 us
    pallas_call x1, Pallas kernels: 124 us -> 118 us  [per_device(): pl.pallas_call(kernel, out_shape=jax.ShapeDtypeStruct((QUAD, 8, WIDTH), f...]
where the time goes in v3:
time: 122 us; the launch traced here: 121 us
  Pallas kernels  118 us (97%)
  local copies, waits for them, and re-layouts  2.89 us (2%)
    pallas_call x1, Pallas kernels, per_device(): pl.pallas_call(kernel, out_shape=jax.ShapeDtypeStruct((QUAD, 8, WIDTH), f...  118 us

profile of v3, /device:TPU:1, one launch (start us, length us, event | category | flops | bytes accessed | tf_op | source)
XLA Modules:
  0.0 121.2 jit_solution(6432684106689745763)
XLA Ops:
  0.0 1.3 %reshape.7.virt_ref = f32[1,1200]{1,0:T(1,128)} reshape(f32[1200]{0:T(1024)} %param.9) | data formatting | bytes 9600 | tf_op jit(solution)/shard_map/reshape | solution.py:467
  1.3 118.3 %shard_map.55 = f32[4,8,1200]{2,1,0:T(8,128)} custom-call(f32[2400,128]{1,0:T(8,128)} %bitcast.3, f32[2,1200,1,1200]{3,2,1,0:T(1,128)} %int_ref.1, f32[4]{0:T(128)} %pair_ref.1, f32[8]{0:T(128)} %block_ref.1, f32[1,1200]{1,0:T(1,128)} %reshape.7.virt_ref), custom_call_target="tpu_custom_call" | custom-call | tf_op jit(solution)/shard_map/pallas_call | solution.py:422
  119.6 1.6 %copy.7 = f32[4,8,1200]{2,1,0:T(8,128)} copy(f32[4,8,1200]{2,1,0:T(8,128)} %shard_map.55) | data formatting | bytes 307200
